TPU v7x, 256 devices: a whole 4x4x8 slice. The times are simulated.
256 devices in a mesh: ctx: 64 (over y, z_lo, x, core), tp: 4 (over z_hi).
Axes of the slice: x: 4, y: 4, z: 8 (z_hi: 4, z_lo: 2; z = z_hi * 2 + z_lo), core: 2. Of those that a mesh axis runs over, the one named last changes fastest.
Arguments:
- queries: bfloat16 [16384, 2048], P('ctx', 'tp'), may hold values from -8 to 8
- span_keys: bfloat16 [16384, 1024], P('ctx', 'tp'), may hold values from -6 to 6
- span_values: bfloat16 [16384, 1024], P('ctx', 'tp'), may hold values from -6 to 6
- cache_keys: bfloat16 [8192, 1024], P('ctx', 'tp'), may hold values from -8 to 8
- cache_values: bfloat16 [8192, 1024], P('ctx', 'tp'), may hold values from -6 to 6
- out_weight: bfloat16 [2048, 3840], P('tp'), may hold values from -0.125 to 0.125
- offsets: int32 [64], replicated, may hold values from 0 to 16128, as said below
- earlier_block_slot: int32 [128], replicated, may hold values from 0 to 127, each once
- prior_block_count: int32 [1], replicated, may hold values from 32 to 127
Outputs:
- projected: bfloat16 [16384, 3840], P('ctx', 'tp')
Inputs may be any that keep to these rules, and one draw needn't show every extreme that they name: `offsets`: a permutation of the multiples of 256 below 16384. Block b of the earlier prompt lies in slot earlier_block_slot[b]; slot s is held by index s // 2 of ctx; only blocks below prior_block_count[0] are valid.
All inputs are finite; a program needn't handle non-finite values.
Results may differ from a plain program's by a relative error of at most 0.012.
Values may be sent and summed in bfloat16 or wider, within the bound.
No kernel may reach another device: no remote copies, remote signals or barrier semaphores. Data moves between devices by JAX's collectives and lax.ppermute only.
A program may use at most 192 MiB of HBM per device.

v0:
```python
import jax
import jax.numpy as jnp
from jax import lax
from jax.sharding import PartitionSpec as P

E = 256
BLK = 64


def per_device(
    queries,
    span_keys,
    span_values,
    cache_keys,
    cache_values,
    out_weight,
    offsets,
    earlier_block_slot,
    prior_block_count,
):
    local_tokens = queries.shape[0]
    kv_local = span_keys.shape[1] // E
    q_local = queries.shape[1] // E
    query_group_width = q_local // kv_local
    query_rows = query_group_width * local_tokens
    shard_count = lax.axis_size("ctx")
    my_shard = lax.axis_index("ctx")
    shard_ids = jnp.arange(shard_count, dtype=jnp.int32)
    my_offset = jnp.sum(jnp.where(shard_ids == my_shard, offsets, 0))
    query_pos = my_offset + jnp.arange(local_tokens, dtype=jnp.int32)
    row_pos = jnp.tile(query_pos, query_group_width)
    slot_count = earlier_block_slot.shape[0]
    slot_ids = jnp.arange(slot_count, dtype=jnp.int32)
    slot_owner_block = jnp.sum(
        jnp.where(earlier_block_slot[None, :] == slot_ids[:, None], slot_ids[None, :], 0), axis=1
    )
    live_slot = slot_owner_block < prior_block_count[0]
    grouped = (
        queries.reshape(local_tokens, kv_local, query_group_width, E)
        .transpose(1, 2, 0, 3)
        .reshape(kv_local, query_rows, E)
    )
    scale = E ** (-0.5)

    def absorb(carry, key_rows, value_rows, allowed):
        largest, total, summed = carry
        new_largest, new_total, new_summed = ([], [], [])
        scores = (
            jnp.einsum("re,ne->rn", grouped[0], key_rows, preferred_element_type=jnp.float32)
            * scale
        )
        scores = jnp.where(allowed, scores, -1e30)
        peak = jnp.maximum(largest[0], jnp.max(scores, axis=1))
        weights = jnp.where(allowed, jnp.exp(scores - peak[:, None]), 0.0)
        factor = jnp.exp(largest[0] - peak)
        new_largest.append(peak)
        new_total.append(total[0] * factor + jnp.sum(weights, axis=1))
        update = jnp.dot(
            weights.astype(jnp.bfloat16), value_rows, preferred_element_type=jnp.float32
        )
        new_summed.append(summed[0] * factor[:, None] + update)
        return (jnp.stack(new_largest), jnp.stack(new_total), jnp.stack(new_summed))

    def guarded(carry, key_rows, value_rows, allowed):
        return absorb(carry, key_rows, value_rows, allowed)

    initial = (
        jnp.full((kv_local, query_rows), -1e30, jnp.float32),
        jnp.zeros((kv_local, query_rows), jnp.float32),
        jnp.zeros((kv_local, query_rows, E), jnp.float32),
    )
    key_rows = lax.all_gather(cache_keys, "ctx", axis=0, tiled=True)
    value_rows = lax.all_gather(cache_values, "ctx", axis=0, tiled=True)
    row_count = key_rows.shape[0]
    slot_number = jnp.arange(row_count, dtype=jnp.int32) // BLK
    allowed = jnp.broadcast_to(
        jnp.any((slot_number[:, None] == slot_ids[None, :]) & live_slot[None, :], axis=1)[None, :],
        (query_rows, row_count),
    )
    state = guarded(initial, key_rows, value_rows, allowed)
    key_rows = lax.all_gather(span_keys, "ctx", axis=0, tiled=True)
    value_rows = lax.all_gather(span_values, "ctx", axis=0, tiled=True)
    row_count = key_rows.shape[0]
    global_row = jnp.arange(row_count, dtype=jnp.int32)
    key_pos = (
        jnp.sum(
            jnp.where(
                (global_row // local_tokens)[:, None] == shard_ids[None, :], offsets[None, :], 0
            ),
            axis=1,
        )
        + global_row % local_tokens
    )
    allowed = key_pos[None, :] <= row_pos[:, None]
    state = guarded(state, key_rows, value_rows, allowed)
    largest, total, summed = state
    attended = summed / total[:, :, None]
    attended = (
        attended.reshape(kv_local, query_group_width, local_tokens, E)
        .transpose(2, 0, 1, 3)
        .reshape(local_tokens, q_local * E)
        .astype(jnp.bfloat16)
    )
    partial_out = jnp.dot(attended, out_weight, preferred_element_type=jnp.float32)
    return lax.psum_scatter(partial_out.astype(jnp.bfloat16), "tp", scatter_dimension=1, tiled=True)


def solution(mesh):
    placed = (
        P("ctx", "tp"),
        P("ctx", "tp"),
        P("ctx", "tp"),
        P("ctx", "tp"),
        P("ctx", "tp"),
        P("tp", None),
        P(),
        P(),
        P(),
    )
    return jax.shard_map(
        per_device, mesh=mesh, in_specs=placed, out_specs=P("ctx", "tp"), check_vma=False
    )
```

profile of v0, /device:TPU:1, one launch (start us, length us, event | category | flops | bytes accessed | tf_op | source)
XLA Modules:
  0.0 531.4 jit_solution(16656678070115511567)
XLA Ops:
  6.5 0.7 all-gather.5.cloned.1.call-update
  7.3 0.7 all-gather.9.cloned.1.call-update
  8.1 0.7 all-gather.7.cloned.1.call-update
  8.8 0.5 all-gather.11.cloned.1.call-update
  9.4 1.3 fusion.39
  10.7 0.6 iota_add_fusion
  11.3 1.1 copy.14
  12.4 0.1 copy.15
  13.2 0.8 select_reduce_fusion.1
  14.0 2.6 fusion.12
  16.6 1.4 select_reduce_fusion
  18.0 103.0 %all-gather.5.cloned.1.call-done = bf16[8192,256]{1,0:T(8,128)(2,1)} async-done(((bf16[128,256]{1,0:T(8,128)(2,1)}), bf16[8192,256]{1,0:T(8,128)(2,1)}) %all-gather.5.cloned.1.call-update) | async-done | bytes 4194320 | tf_op jit(solution)/shard_map/all_gather | solution.py:72
  121.0 9.4 %fusion.5 = (f32[512]{0:T(512)S(1)}, f32[512,8192]{1,0:T(8,128)}) fusion(pred[8192]{0:T(1024)(128)(4,1)S(1)} %fusion.12, bf16[512,256]{1,0:T(8,128)(2,1)S(1)} %bitcast.23, bf16[8192,256]{1,0:T(8,128)(2,1)} %all-gather.5.cloned.1.call-done), kind=kOutput, calls=%fused_computation.8 | convolution fusion | flops 2160066048 | bytes 21243904 | tf_op jit(solution)/shard_map/re,ne->rn/dot_general | solution.py:49
  130.4 104.0 %all-gather.9.cloned.1.call-done = bf16[16384,256]{1,0:T(8,128)(2,1)} async-done(((bf16[256,256]{1,0:T(8,128)(2,1)}), bf16[16384,256]{1,0:T(8,128)(2,1)}) %all-gather.9.cloned.1.call-update) | async-done | bytes 8388624 | tf_op jit(solution)/shard_map/all_gather | solution.py:81
  234.4 17.2 %fusion = (f32[512]{0:T(512)S(1)}, f32[512,16384]{1,0:T(8,128)}) fusion(s32[16384]{0:T(1024)S(1)} %fusion.34, s32[512]{0:T(512)S(1)} %bitcast.26, bf16[512,256]{1,0:T(8,128)(2,1)S(1)} %bitcast.24, bf16[16384,256]{1,0:T(8,128)(2,1)} %all-gather.9.cloned.1.call-done), kind=kOutput, calls=%fused_computation.2 | convolution fusion | flops 4328521216 | bytes 42274816 | tf_op jit(solution)/shard_map/re,ne->rn/dot_general | solution.py:49
  251.6 8.6 %fusion.6 = f32[512]{0:T(512)S(1)} fusion(f32[512,8192]{1,0:T(8,128)} %get-tuple-element.11, f32[512]{0:T(512)S(1)} %get-tuple-element.9, pred[8192]{0:T(1024)(128)(4,1)S(1)} %fusion.12), kind=kLoop, calls=%fused_computation.9 | loop fusion | flops 20971008 | bytes 16789504 | tf_op jit(solution)/shard_map/reduce_sum | solution.py:57
  260.2 15.9 %fusion.1 = f32[512]{0:T(512)S(1)} fusion(f32[512,16384]{1,0:T(8,128)} %get-tuple-element.13, f32[512]{0:T(512)S(1)} %get-tuple-element.8, s32[16384]{0:T(1024)S(1)} %fusion.34, s32[512]{0:T(512)S(1)} %bitcast.27), kind=kLoop, calls=%fused_computation.3 | loop fusion | flops 50331136 | bytes 33626112 | tf_op jit(solution)/shard_map/reduce_sum | solution.py:57
  276.1 66.8 %all-gather.7.cloned.1.call-done = bf16[8192,256]{1,0:T(8,128)(2,1)} async-done(((bf16[128,256]{1,0:T(8,128)(2,1)}), bf16[8192,256]{1,0:T(8,128)(2,1)}) %all-gather.7.cloned.1.call-update) | async-done | bytes 4194320 | tf_op jit(solution)/shard_map/all_gather | solution.py:73
  342.9 8.8 %fusion.19 = f32[512,256]{1,0:T(8,128)S(1)} fusion(bf16[8192,256]{1,0:T(8,128)(2,1)} %all-gather.7.cloned.1.call-done, f32[512,8192]{1,0:T(8,128)} %get-tuple-element.11, f32[512]{0:T(512)S(1)} %get-tuple-element.9, pred[8192]{0:T(1024)(128)(4,1)S(1)} %fusion.12, f32[512]{0:T(512)S(1)} %get-tuple-element.6, f32[512]{0:T(512)S(1)} %get-tuple-element.7), kind=kOutput, calls=%fused_computation.21 | convolution fusion | flops 2168717312 | bytes 21510144 | tf_op jit(solution)/shard_map/dot_general | solution.py:58
  351.7 104.4 %all-gather.11.cloned.1.call-done = bf16[16384,256]{1,0:T(8,128)(2,1)} async-done(((bf16[256,256]{1,0:T(8,128)(2,1)}), bf16[16384,256]{1,0:T(8,128)(2,1)}) %all-gather.11.cloned.1.call-update) | async-done | bytes 8388624 | tf_op jit(solution)/shard_map/all_gather | solution.py:82
  456.1 16.8 %fusion.25 = bf16[512,256]{1,0:T(8,128)(2,1)S(1)} fusion(f32[512,256]{1,0:T(8,128)S(1)} %fusion.19, bf16[16384,256]{1,0:T(8,128)(2,1)} %all-gather.11.cloned.1.call-done, f32[512,16384]{1,0:T(8,128)} %get-tuple-element.13, f32[512]{0:T(512)S(1)} %get-tuple-element.8, s32[16384]{0:T(1024)S(1)} %fusion.34, s32[512]{0:T(512)S(1)} %bitcast.28, ...), kind=kOutput, calls=%fused_computation.23 | convolution fusion | flops 4345692160 | bytes 42801152 | tf_op jit(solution)/shard_map/dot_general | solution.py:58
  472.9 0.1 copy.16
  473.0 5.0 convolution_convert_fusion
  478.1 46.8 %reduce-scatter.2.cloned.1.call-done = bf16[256,960]{0,1:T(8,128)(2,1)} async-done(((bf16[256,3840]{0,1:T(8,128)(2,1)}), bf16[256,960]{0,1:T(8,128)(2,1)}) %reduce-scatter.2.cloned.1.call-update) | async-done | bytes 491536 | tf_op jit(solution)/shard_map/reduce_scatter | solution.py:105
  (14 shorter events, 0.2 us)
Async XLA Ops:
  6.5 114.5 %all-gather.5.cloned.1.call-start = ((), (), s32[]{:S(2)}) async-start(), calls=%async_computation.1 | async-start | bytes 4259840 | tf_op jit(solution)/shard_map/all_gather | solution.py:72
  7.3 227.1 %all-gather.9.cloned.1.call-start = ((), (), s32[]{:S(2)}) async-start(), calls=%async_computation.3 | async-start | bytes 8519680 | tf_op jit(solution)/shard_map/all_gather | solution.py:81
  8.0 334.9 %all-gather.7.cloned.1.call-start = ((), (), s32[]{:S(2)}) async-start(), calls=%async_computation.2 | async-start | bytes 4259840 | tf_op jit(solution)/shard_map/all_gather | solution.py:73
  8.7 447.4 %all-gather.11.cloned.1.call-start = ((), (), s32[]{:S(2)}) async-start(), calls=%async_computation.4 | async-start | bytes 8519680 | tf_op jit(solution)/shard_map/all_gather | solution.py:82
  9.3 515.6 %reduce-scatter.2.cloned.1.call-start = ((), (), s32[]{:S(2)}) async-start(), calls=%async_computation.5 | async-start | bytes 2457600 | tf_op jit(solution)/shard_map/reduce_scatter | solution.py:105
Sparse Core Ops, SparseCore 0:
  9.2 111.7 all-gather.4
  122.9 111.4 all-gather.8
  236.3 106.5 all-gather.6
  344.6 111.4 all-gather.10
  478.2 46.6 reduce-scatter.1
where the time goes:
time: 532 us; the launch traced here: 531 us
  waiting for transfers between devices  428 us (80%)
  matrix products  57.2 us (11%)
  other arithmetic  31.2 us (6%)
  between operations  13.9 us (3%)
    all_gather x1, waiting for transfers between devices, per_device(): value_rows = lax.all_gather(span_values, 'ctx', axis=0, tiled=True)  104 us
    all_gather x1, waiting for transfers between devices, per_device(): key_rows = lax.all_gather(span_keys, 'ctx', axis=0, tiled=True)  104 us
    all_gather x1, waiting for transfers between devices, per_device(): key_rows = lax.all_gather(cache_keys, 'ctx', axis=0, tiled=True)  103 us
    all_gather x1, waiting for transfers between devices, per_device(): value_rows = lax.all_gather(cache_values, 'ctx', axis=0, tiled=True)  66.8 us
    reduce_scatter x1, waiting for transfers between devices, per_device(): lax.psum_scatter(partial_out.astype(jnp.bfloat16), 'tp', scatter_dimensio...  46.8 us
    dot_general x2, matrix products, absorb(): jnp.einsum('re,ne->rn', grouped[0], key_rows, preferred_element_type=jnp....  26.6 us
    dot_general x2, matrix products, absorb(): jnp.dot(weights.astype(jnp.bfloat16), value_rows, preferred_element_type=...  25.6 us
    reduce_sum x2, other arithmetic, absorb(): new_total.append(total[0] * factor + jnp.sum(weights, axis=1))  24.5 us
  transfers between devices with their start and end apart: 5, of which 5 were waited for; matrix products, arithmetic and copies ran while one was open for 13% of the time, Pallas kernels for 0%

commit v1 on v0

--- a/solution.py
+++ b/solution.py
@@ -69,8 +69,13 @@
         jnp.zeros((kv_local, query_rows), jnp.float32),
         jnp.zeros((kv_local, query_rows, E), jnp.float32),
     )
-    key_rows = lax.all_gather(cache_keys, "ctx", axis=0, tiled=True)
-    value_rows = lax.all_gather(cache_values, "ctx", axis=0, tiled=True)
+    key_rows, value_rows = jnp.split(
+        lax.all_gather(
+            jnp.concatenate([cache_keys, cache_values], axis=1), "ctx", axis=0, tiled=True
+        ),
+        [cache_keys.shape[1]],
+        axis=1,
+    )
     row_count = key_rows.shape[0]
     slot_number = jnp.arange(row_count, dtype=jnp.int32) // BLK
     allowed = jnp.broadcast_to(

time: 532 us -> 429 us (0.81)
  waiting for transfers between devices: 428 us -> 324 us
    all_gather x2 -> x1, waiting for transfers between devices: 170 us -> 108 us  [per_device(): lax.all_gather(jnp.concatenate([cache_keys, cache_values], axis=1), 'ctx'...]
    all_gather x1, waiting for transfers between devices: 104 us -> 63.4 us  [per_device(): value_rows = lax.all_gather(span_values, 'ctx', axis=0, tiled=True)]
  transfers between devices with their start and end apart: 5 -> 4, of which waited for: 5 -> 4; matrix products, arithmetic and copies ran while one was open for 13% -> 16% of each run, Pallas kernels for 0% -> 0%
where the time goes in v1:
time: 429 us
  waiting for transfers between devices  324 us (76%)
  matrix products  53.9 us (13%)
  other arithmetic  35.4 us (8%)
  between operations  14 us (3%)
    all_gather x1, waiting for transfers between devices, per_device(): lax.all_gather(jnp.concatenate([cache_keys, cache_values], axis=1), 'ctx'...  108 us
    all_gather x1, waiting for transfers between devices, per_device(): key_rows = lax.all_gather(span_keys, 'ctx', axis=0, tiled=True)  104 us
    all_gather x1, waiting for transfers between devices, per_device(): value_rows = lax.all_gather(span_values, 'ctx', axis=0, tiled=True)  63.4 us
    reduce_scatter x1, waiting for transfers between devices, per_device(): lax.psum_scatter(partial_out.astype(jnp.bfloat16), 'tp', scatter_dimensio...  46.8 us
    reduce_sum x2, other arithmetic, absorb(): new_total.append(total[0] * factor + jnp.sum(weights, axis=1))  27.1 us
    dot_general x2, matrix products, absorb(): jnp.einsum('re,ne->rn', grouped[0], key_rows, preferred_element_type=jnp....  26.5 us
    dot_general x2, matrix products, absorb(): jnp.dot(weights.astype(jnp.bfloat16), value_rows, preferred_element_type=...  22.3 us
  transfers between devices with their start and end apart: 4, of which 4 were waited for; matrix products, arithmetic and copies ran while one was open for 16% of the time, Pallas kernels for 0%

profile of v1, /device:TPU:1, one launch (start us, length us, event | category | flops | bytes accessed | tf_op | source)
XLA Modules:
  0.0 428.6 jit_solution(16611576830803351531)
XLA Ops:
  6.5 1.5 pad_maximum_fusion
  8.1 0.0 all-gather.6.cloned.1.call-start
  8.1 0.7 all-gather.6.cloned.1.call-update
  8.9 0.7 all-gather.8.cloned.1.call-update
  9.6 0.0 reduce-scatter.2.cloned.1.call-start
  9.6 1.3 fusion.46
  11.0 0.6 iota_add_fusion
  11.6 1.1 copy.14
  12.7 0.1 copy.15
  13.5 0.8 select_reduce_fusion.1
  14.3 2.6 fusion.15
  16.9 1.4 select_reduce_fusion
  18.3 107.9 %all-gather.4.cloned.1.call-done = bf16[8192,512]{1,0:T(8,128)(2,1)} async-done(((bf16[128,512]{1,0:T(8,128)(2,1)}), bf16[8192,512]{1,0:T(8,128)(2,1)}) %all-gather.4.cloned.1.call-update) | async-done | bytes 8388624 | tf_op jit(solution)/shard_map/all_gather | solution.py:73
  126.2 9.2 %fusion.5 = (f32[512]{0:T(512)S(1)}, f32[8192,512]{1,0:T(8,128)}) fusion(pred[8192]{0:T(1024)(128)(4,1)S(1)} %fusion.15, bf16[512,256]{1,0:T(8,128)(2,1)S(1)} %bitcast.23, bf16[8192,512]{1,0:T(8,128)(2,1)} %all-gather.4.cloned.1.call-done), kind=kOutput, calls=%fused_computation.8 | convolution fusion | flops 2160066048 | bytes 21243904 | tf_op jit(solution)/shard_map/re,ne->rn/dot_general | solution.py:49
  135.4 104.4 %all-gather.6.cloned.1.call-done = bf16[16384,256]{1,0:T(8,128)(2,1)} async-done(((bf16[256,256]{1,0:T(8,128)(2,1)}), bf16[16384,256]{1,0:T(8,128)(2,1)}) %all-gather.6.cloned.1.call-update) | async-done | bytes 8388624 | tf_op jit(solution)/shard_map/all_gather | solution.py:86
  239.8 17.3 %fusion = (f32[512]{0:T(512)S(1)}, f32[512,16384]{1,0:T(8,128)}) fusion(s32[16384]{0:T(1024)S(1)} %fusion.41, s32[512]{0:T(512)S(1)} %bitcast.26, bf16[512,256]{1,0:T(8,128)(2,1)S(1)} %bitcast.24, bf16[16384,256]{1,0:T(8,128)(2,1)} %all-gather.6.cloned.1.call-done), kind=kOutput, calls=%fused_computation.2 | convolution fusion | flops 4328521216 | bytes 42274816 | tf_op jit(solution)/shard_map/re,ne->rn/dot_general | solution.py:49
  257.1 9.6 %fusion.6 = f32[512]{0:T(512)S(1)} fusion(f32[8192,512]{1,0:T(8,128)} %get-tuple-element.11, f32[512]{0:T(512)S(1)} %get-tuple-element.9, pred[8192]{0:T(1024)(128)(4,1)S(1)} %fusion.15), kind=kLoop, calls=%fused_computation.9 | loop fusion | flops 20971008 | bytes 16789504 | tf_op jit(solution)/shard_map/reduce_sum | solution.py:57
  266.8 17.5 %fusion.1 = f32[512]{0:T(512)S(1)} fusion(f32[512,16384]{1,0:T(8,128)} %get-tuple-element.13, f32[512]{0:T(512)S(1)} %get-tuple-element.8, s32[16384]{0:T(1024)S(1)} %fusion.41, s32[512]{0:T(512)S(1)} %bitcast.27), kind=kLoop, calls=%fused_computation.3 | loop fusion | flops 50331136 | bytes 33626112 | tf_op jit(solution)/shard_map/reduce_sum | solution.py:57
  284.4 5.5 %fusion.24 = f32[512,256]{1,0:T(8,128)S(1)} fusion(bf16[8192,512]{1,0:T(8,128)(2,1)S(1)} %bitcast.30, f32[8192,512]{1,0:T(8,128)S(1)} %bitcast.20, f32[512]{0:T(512)S(1)} %get-tuple-element.9, pred[8192]{0:T(1024)(128)(4,1)S(1)} %fusion.15, f32[512]{0:T(512)S(1)} %get-tuple-element.6, f32[512]{0:T(512)S(1)} %get-tuple-element.7), kind=kOutput, calls=%fused_computation.24 | convolution fusion | flops 2168717312 | bytes 21510144 | tf_op jit(solution)/shard_map/dot_general | solution.py:58
  290.0 63.4 %all-gather.8.cloned.1.call-done = bf16[16384,256]{1,0:T(8,128)(2,1)} async-done(((bf16[256,256]{1,0:T(8,128)(2,1)}), bf16[16384,256]{1,0:T(8,128)(2,1)}) %all-gather.8.cloned.1.call-update) | async-done | bytes 8388624 | tf_op jit(solution)/shard_map/all_gather | solution.py:87
  353.4 16.8 %fusion.32 = bf16[512,256]{1,0:T(8,128)(2,1)S(1)} fusion(f32[512,256]{1,0:T(8,128)S(1)} %fusion.24, bf16[16384,256]{1,0:T(8,128)(2,1)} %all-gather.8.cloned.1.call-done, f32[512,16384]{1,0:T(8,128)} %get-tuple-element.13, f32[512]{0:T(512)S(1)} %get-tuple-element.8, s32[16384]{0:T(1024)S(1)} %fusion.41, s32[512]{0:T(512)S(1)} %bitcast.28, ...), kind=kOutput, calls=%fused_computation.26 | convolution fusion | flops 4345692160 | bytes 42801152 | tf_op jit(solution)/shard_map/dot_general | solution.py:58
  370.1 0.1 copy.16
  370.3 5.0 %convolution_convert_fusion = bf16[256,3840]{0,1:T(8,128)(2,1)} fusion(bf16[256,512]{0,1:T(8,128)(2,1)S(1)} %bitcast.21, bf16[512,3840]{1,0:T(8,128)(2,1)} %param.14), kind=kOutput, calls=%fused_computation.13 | convolution fusion | flops 1007616000 | bytes 6160384 | tf_op jit(solution)/shard_map/dot_general | solution.py:109
  375.3 46.8 %reduce-scatter.2.cloned.1.call-done = bf16[256,960]{0,1:T(8,128)(2,1)} async-done(((bf16[256,3840]{0,1:T(8,128)(2,1)}), bf16[256,960]{0,1:T(8,128)(2,1)}) %reduce-scatter.2.cloned.1.call-update) | async-done | bytes 491536 | tf_op jit(solution)/shard_map/reduce_scatter | solution.py:110
  (26 shorter events, 0.2 us)
Async XLA Ops:
  6.5 119.6 %all-gather.4.cloned.1.call-start = ((), (), s32[]{:S(2)}) async-start(), calls=%async_computation.1 | async-start | bytes 8519680 | tf_op jit(solution)/shard_map/all_gather | solution.py:73
  8.1 231.7 %all-gather.6.cloned.1.call-start = ((), (), s32[]{:S(2)}) async-start(), calls=%async_computation.2 | async-start | bytes 8519680 | tf_op jit(solution)/shard_map/all_gather | solution.py:86
  8.8 344.5 %all-gather.8.cloned.1.call-start = ((), (), s32[]{:S(2)}) async-start(), calls=%async_computation.3 | async-start | bytes 8519680 | tf_op jit(solution)/shard_map/all_gather | solution.py:87
  9.6 412.5 %reduce-scatter.2.cloned.1.call-start = ((), (), s32[]{:S(2)}) async-start(), calls=%async_computation.4 | async-start | bytes 2457600 | tf_op jit(solution)/shard_map/reduce_scatter | solution.py:110
  257.1 27.2 %slice-start = ((s8[16777216]{0:T(1024)(128)(4,1)}), s8[4194304]{0:T(1024)(128)(4,1)S(1)}, s32[]{:S(2)}) async-start(s8[16777216]{0:T(1024)(128)(4,1)} %bitcast.19), calls=%async_computation.5 | async-start | bytes 8388608
  257.1 27.2 %slice-start.1 = ((s8[16777216]{0:T(1024)(128)(4,1)}), s8[4194304]{0:T(1024)(128)(4,1)S(1)}, s32[]{:S(2)}) async-start(s8[16777216]{0:T(1024)(128)(4,1)} %bitcast.19), calls=%async_computation.6 | async-start | bytes 8388608
  257.1 27.2 %slice-start.4 = ((s8[8388608]{0:T(1024)(128)(4,1)}), s8[4194304]{0:T(1024)(128)(4,1)S(1)}, s32[]{:S(2)}) async-start(s8[8388608]{0:T(1024)(128)(4,1)} %bitcast.29), calls=%async_computation.9 | async-start | bytes 8388608
  266.8 17.6 %slice-start.2 = ((s8[16777216]{0:T(1024)(128)(4,1)}), s8[4194304]{0:T(1024)(128)(4,1)S(1)}, s32[]{:S(2)}) async-start(s8[16777216]{0:T(1024)(128)(4,1)} %bitcast.19), calls=%async_computation.7 | async-start | bytes 8388608
  266.8 17.6 %slice-start.3 = ((s8[16777216]{0:T(1024)(128)(4,1)}), s8[4194304]{0:T(1024)(128)(4,1)S(1)}, s32[]{:S(2)}) async-start(s8[16777216]{0:T(1024)(128)(4,1)} %bitcast.19), calls=%async_computation.8 | async-start | bytes 8388608
  266.8 17.6 %slice-start.5 = ((s8[8388608]{0:T(1024)(128)(4,1)}), s8[4194304]{0:T(1024)(128)(4,1)S(1)}, s32[]{:S(2)}) async-start(s8[8388608]{0:T(1024)(128)(4,1)} %bitcast.29), calls=%async_computation.10 | async-start | bytes 8388608
Sparse Core Ops, SparseCore 0:
  9.2 116.9 all-gather.3
  128.0 111.6 all-gather.5
  241.6 111.6 all-gather.7
  375.4 46.6 reduce-scatter.1
